TPU v7x, 32 devices: a whole 2x2x4 slice. The times are simulated.
32 devices in a mesh: col: 4 (over z), row: 8 (over y, x, core).
Axes of the slice: x: 2, y: 2, z: 4, core: 2. Of those that a mesh axis runs over, the one named last changes fastest.
Arguments:
- matrix: float32 [8192, 8192], P('row', 'col'), may hold values from -6 to 6
- pattern: int32 [32, 4], P('row'), may hold values 0 or 1
- active: int32 [8, 4, 24, 2], P('row', 'col'), may hold values from 0 to 7, as said below
- pivots: int32 [4], replicated, may hold values from 0 to 31, as said below
- lower_inv: float32 [4, 256, 256], replicated, may hold values from -0.3 to 0.3, as said below
- upper_inv: float32 [4, 256, 256], replicated, may hold values from -0.3 to 0.3, as said below
Outputs:
- factored: float32 [8192, 8192], P('row', 'col')
Inputs may be any that keep to these rules, and one draw needn't show every extreme that they name: For each device (a, b), active[a, b] holds 24 distinct pairs (l, c) with l below 4 and c below 8. `pivots`: 4 distinct block rows of the window, among them always the first and the last block row. `lower_inv`: each block is lower triangular with a positive diagonal. `upper_inv`: each block is upper triangular with a positive diagonal.
All inputs are finite; a program needn't handle non-finite values. No bound on the sum of `pattern` on one device may be relied on, other than what follows from the above.
Results may differ from a plain program's by a relative error of at most 0.0001.
Values sent between devices are 32-bit elements; how exact they have to be, the bound alone decides.
A program may use at most 128 MiB of HBM per device.

v0:
```python
import functools

import jax
import jax.numpy as jnp
from jax import lax
from jax.experimental import pallas as pl
from jax.experimental.pallas import tpu as pltpu
from jax.sharding import PartitionSpec as P


def when(cond, fn):
    pl.when(cond)(fn)


def loop(low, high, fn):
    def one(index, carry):
        fn(index)
        return carry

    lax.fori_loop(low, high, one, 0)


def ranked(piv):
    a, b = jnp.minimum(piv[0], piv[1]), jnp.maximum(piv[0], piv[1])
    c, d = jnp.minimum(piv[2], piv[3]), jnp.maximum(piv[2], piv[3])
    e, f = jnp.maximum(a, c), jnp.minimum(b, d)
    return jnp.minimum(e, f), jnp.maximum(e, f)


def comm_kernel(
    dims, axes, hits, meta, mat, rows, strips, cross, metas,
    matv, send1, recv1, buf2, recv2, homev,
    m_send, m_recv, z_send, z_recv, ab_send, ab_recv, one_send, one_recv,
    two_send, two_recv, ag_send, ag_recv, xs_send, xs_recv, xz_send, xz_recv, local,
):
    panels, tile, r_loc, width, rsize, csize = dims
    chips = rsize // 2
    w = width // rsize
    rr = tile // rsize
    holders = tile // w
    last = panels - 1
    me = lax.axis_index("row")
    plane = lax.axis_index("col")
    chip, core = me // 2, me % 2
    lin = plane * rsize + me
    square = chips == 4

    def dev(row, col):
        return tuple(row if name == "row" else col for name in axes)

    def remote(src, dst, ssem, rsem, row, col):
        return pltpu.make_async_remote_copy(
            src_ref=src, dst_ref=dst, send_sem=ssem, recv_sem=rsem,
            device_id=dev(row, col), device_id_type=pl.DeviceIdType.MESH,
        )

    if square:
        x, y = chip % 2, chip // 2
        xn, yn = chip + 1 - 2 * x, chip + 2 - 4 * y
        to_chip = from_chip = [xn, yn, 3 - chip]
    else:
        to_chip = [(chip + d) % chips for d in range(1, chips)]
        from_chip = [(chip - d + chips) % chips for d in range(1, chips)]
    sib = chip * 2 + 1 - core

    def meta_copy(t):
        return remote(meta, metas.at[lin], m_send.at[t], m_recv.at[lin], t % rsize, t // rsize)

    def meta_in(t):
        return remote(meta, metas.at[t], m_send.at[t], m_recv.at[t], t % rsize, t // rsize)

    loop(0, rsize * csize, lambda t: when(t != lin, lambda: meta_copy(t).start()))
    own_meta = pltpu.make_async_copy(meta, metas.at[lin], local.at[0])
    own_meta.start()

    def z_rows(r):
        return pl.ds(pl.multiple_of(r * tile, tile), tile)

    def z_own(r, up):
        return remote(
            mat.at[z_rows(r), pl.ds(0, tile)], strips.at[plane, z_rows(r)],
            z_send.at[1 - up, plane, r], z_recv.at[1 - up, plane, r], me, plane + 2 * up - 1,
        )

    def z_pass(n, r, up):
        return remote(
            strips.at[n, z_rows(r)], strips.at[n, z_rows(r)],
            z_send.at[1 - up, n, r], z_recv.at[1 - up, n, r], me, plane + 2 * up - 1,
        )

    is_holder = plane < panels

    def z_start(r):
        when(is_holder & (plane + 1 < csize), lambda: z_own(r, 1).start())
        when(is_holder & (plane > 0), lambda: z_own(r, 0).start())

    loop(0, r_loc, z_start)

    def z_relay(p, r):
        low, high = plane - p, plane + p

        def from_low():
            z_pass(low, r, 1).wait_recv()
            when(plane + 1 < csize, lambda: z_pass(low, r, 1).start())

        def from_high():
            z_pass(high, r, 0).wait_recv()
            when(plane > 0, lambda: z_pass(high, r, 0).start())

        when((low >= 0) & (low < panels), from_low)
        when(high < panels, from_high)

    def z_drain(p, r):
        low, high = plane - p, plane + p
        if p == 0:
            when(is_holder & (plane + 1 < csize), lambda: z_own(r, 1).wait_send())
            when(is_holder & (plane > 0), lambda: z_own(r, 0).wait_send())
        else:
            when((low >= 0) & (low < panels) & (plane + 1 < csize), lambda: z_pass(low, r, 1).wait_send())
            when((high < panels) & (plane > 0), lambda: z_pass(high, r, 0).wait_send())

    load = pltpu.make_async_copy(mat, matv, local.at[1])
    load.start()

    def cols_at(a):
        return pl.ds(pl.multiple_of(a * w, w), w)

    def fixed(slot, root):
        base = 0 if slot == 0 else (r_loc - 1) * tile

        def to(a):
            return remote(
                mat.at[pl.ds(base, tile), cols_at(a)], rows.at[a, slot],
                ab_send.at[slot, a], ab_recv.at[slot], a, plane,
            )

        return to

    top, bottom = fixed(0, 0), fixed(last, rsize - 1)
    when(me == 0, lambda: loop(1, rsize, lambda a: top(a).start()))
    when(me == rsize - 1, lambda: loop(0, rsize - 1, lambda a: bottom(a).start()))

    load.wait()
    high_core = (core == 0).astype(jnp.float32)
    low_core = 1.0 - high_core
    step = 32

    def one(s):
        return remote(send1.at[s], recv1.at[s], one_send.at[s], one_recv.at[s], sib, plane)

    def pick(part):
        at = pl.ds(pl.multiple_of(part * step, step), step)
        for q in range(chips):
            even, odd = [], []
            for r in range(r_loc):
                there = pl.ds(pl.multiple_of(r * tile + part * step, step), step)
                even.append(matv[there, 2 * q * w : (2 * q + 1) * w])
                odd.append(matv[there, (2 * q + 1) * w : (2 * q + 2) * w])
            for s in range(2):
                left = sum(even[r] * hits[s, r] for r in range(r_loc))
                right = sum(odd[r] * hits[s, r] for r in range(r_loc))
                send1[s, q, at] = left * low_core + right * high_core
                buf2[s, q, at] = left * high_core + right * low_core

    loop(0, tile // step, pick)
    for s in range(2):
        one(s).start()
    own_slot = pltpu.make_async_copy(matv.at[pl.ds(0, tile), pl.ds(0, w)], rows.at[0, 0], local.at[2])
    own_last = pltpu.make_async_copy(
        matv.at[pl.ds((r_loc - 1) * tile, tile), pl.ds((rsize - 1) * w, w)], rows.at[rsize - 1, last], local.at[2]
    )
    own_strip = pltpu.make_async_copy(matv.at[:, pl.ds(0, tile)], strips.at[plane], local.at[3])
    when(me == 0, lambda: own_slot.start())
    when(me == rsize - 1, lambda: own_last.start())
    when(is_holder, lambda: own_strip.start())

    def two(s, d):
        return remote(
            buf2.at[s, to_chip[d]], recv2.at[s, d], two_send.at[s, d], two_recv.at[s, d],
            to_chip[d] * 2 + core, plane,
        )

    for s in range(2):
        one(s).wait_recv()
        for q in range(chips):
            buf2[s, q] = buf2[s, q] + recv1[s, q]
        for d in range(chips - 1):
            two(s, d).start()
    for r in range(2):
        z_relay(1, r)

    def region(a, c):
        return rows.at[a, c]

    def x_region(a, n):
        return cross.at[n, :, pl.ds(pl.multiple_of(a * rr, rr), rr), :]

    def ag(part, c, kind, a, row):
        ref = region(a, c) if part == 0 else x_region(a, c)
        return remote(ref, ref, ag_send.at[part, kind, c], ag_recv.at[part, kind, c], row, plane)

    direct = 2 if square else chips - 1
    sib_own = chips - 1

    def ag_start(part, c):
        ag(part, c, sib_own, me, sib).start()
        for d in range(direct):
            ag(part, c, d, me, to_chip[d] * 2 + core).start()

    def ag_own_wait(part, c):
        ag(part, c, sib_own, me, sib).wait_send()
        for d in range(direct):
            ag(part, c, d, me, to_chip[d] * 2 + core).wait_send()

    def peer(d):
        return from_chip[d] * 2 + core

    def ag_forward(part, c, first):
        for d in range(direct):
            ag(part, c, d, peer(d), sib).wait_recv()
            if square and first == (d == 0):
                ag(part, c, 2, peer(d), to_chip[1 - d] * 2 + core).start()
            ag(part, c, chips + d, peer(d), sib).start()

    def ag_far(part, c):
        if square:
            ag(part, c, 2, peer(2), sib).wait_recv()
            ag(part, c, chips + 2, peer(2), sib).start()

    def ag_end(part, c, first):
        for d in range(chips):
            kind = sib_own if d == chips - 1 else chips + d
            ag(part, c, kind, sib if d == chips - 1 else from_chip[d] * 2 + 1 - core, sib).wait_recv()
        ag_own_wait(part, c)
        for d in range(chips - 1):
            ag(part, c, chips + d, peer(d), sib).wait_send()
        if square:
            d = 0 if first else 1
            ag(part, c, 2, peer(d), to_chip[1 - d] * 2 + core).wait_send()

    def fixed_in(slot, root, own):
        when(me != root, lambda: (top if slot == 0 else bottom)(me).wait_recv())
        when(me == root, lambda: own.wait())

    for s in range(2):
        acc = buf2[s, chip]
        for d in range(chips - 1):
            two(s, d).wait_recv()
            acc = acc + recv2[s, d]
        homev[s] = acc
        put = pltpu.make_async_copy(homev.at[s], rows.at[me, s + 1], local.at[4 + s])
        put.start()
        put.wait()
        ag_start(0, s + 1)
        if s == 0:
            fixed_in(0, 0, own_slot)
            ag_start(0, 0)
            z_relay(1, 2)
        else:
            fixed_in(last, rsize - 1, own_last)
            ag_start(0, last)
            loop(3, r_loc, lambda r: z_relay(1, r))

    def xs(h, a):
        return remote(
            rows.at[h, :, pl.ds(pl.multiple_of(a * rr, rr), rr), :],
            cross.at[plane, :, pl.ds(pl.multiple_of(a * rr, rr), rr), pl.ds(h * w, w)],
            xs_send.at[h, a], xs_recv.at[h], a, plane,
        )

    for h in range(holders):
        own_x = pltpu.make_async_copy(
            rows.at[h, :, pl.ds(h * rr, rr), :],
            cross.at[plane, :, pl.ds(h * rr, rr), pl.ds(h * w, w)], local.at[6 + h],
        )

        def give(h=h, own_x=own_x):
            own_x.start()
            loop(0, rsize, lambda a: when(a != h, lambda: xs(h, a).start()))

        def take(h=h, own_x=own_x):
            when(me == h, lambda: own_x.wait())
            when(me != h, lambda: xs(h, me).wait_recv())

        when(is_holder & (me == h), give)
        when(is_holder, take)

    def xz(d):
        return remote(
            x_region(me, plane), x_region(me, plane), xz_send.at[d], xz_recv.at[plane],
            me, (plane + d) % csize,
        )

    when(is_holder, lambda: loop(1, csize, lambda d: xz(d).start()))

    half = panels // 2
    loop(0, half, lambda c: ag_forward(0, c, True))
    loop(half, panels, lambda c: ag_forward(0, c, False))
    for p in range(2, csize):
        loop(0, r_loc, lambda r, p=p: z_relay(p, r))

    def x_start(n):
        got = remote(x_region(me, n), x_region(me, n), xz_send.at[0], xz_recv.at[n], me, plane)
        when(plane != n, lambda: got.wait_recv())
        ag_start(1, n)

    loop(0, panels, x_start)
    loop(0, panels, lambda c: ag_far(0, c))
    loop(0, half, lambda c: ag_forward(1, c, True))
    loop(half, panels, lambda c: ag_forward(1, c, False))
    loop(0, panels, lambda c: ag_far(1, c))
    for part in range(2):
        loop(0, half, lambda c: ag_end(part, c, True))
        loop(half, panels, lambda c: ag_end(part, c, False))
    for p in range(csize):
        loop(0, r_loc, lambda r, p=p: z_drain(p, r))
    when(is_holder, lambda: loop(1, csize, lambda d: xz(d).wait_send()))
    for h in range(holders):
        when(
            is_holder & (me == h),
            lambda h=h: loop(0, rsize, lambda a: when(a != h, lambda: xs(h, a).wait_send())),
        )
    for s in range(2):
        one(s).wait_send()
        for d in range(chips - 1):
            two(s, d).wait_send()
    when(me == 0, lambda: loop(1, rsize, lambda a: top(a).wait_send()))
    when(me == rsize - 1, lambda: loop(0, rsize - 1, lambda a: bottom(a).wait_send()))
    when(is_holder, lambda: own_strip.wait())
    own_meta.wait()

    def meta_end(t):
        meta_copy(t).wait_send()
        meta_in(t).wait_recv()

    loop(0, rsize * csize, lambda t: when(t != lin, lambda: meta_end(t)))


def halves(value):
    high = value.astype(jnp.bfloat16)
    return high, (value - high.astype(jnp.float32)).astype(jnp.bfloat16)


def dot(left, right):
    return jnp.dot(left, right, preferred_element_type=jnp.float32)


def mm(left, right):
    (ah, al), (bh, bl) = left, right
    return dot(ah, bh) + dot(ah, bl) + dot(al, bh)


def lu_kernel(
    dims, piv, metas, mat, rows, strips, cross, linv, uinv, out,
    matv, rowv, stripv, crossv, lv, uv, linvs, uinvs, lows, ups, us, ls, lf, slot, sems, mat_sem,
):
    panels, tile, r_loc, width, rsize, csize = dims
    c_loc = width // tile
    w = width // rsize
    cells = r_loc * c_loc
    me = lax.axis_index("row")
    plane = lax.axis_index("col")

    def tile_at(ref, i, j):
        return ref.at[pl.ds(pl.multiple_of(i * tile, tile), tile), pl.ds(pl.multiple_of(j * tile, tile), tile)]

    loads = [
        pltpu.make_async_copy(cross, crossv, sems.at[0]),
        pltpu.make_async_copy(linv, lv, sems.at[1]),
        pltpu.make_async_copy(uinv, uv, sems.at[2]),
        pltpu.make_async_copy(strips, stripv, sems.at[3]),
    ]
    for load in loads:
        load.start()
    row_loads = []
    for a in range(rsize):
        j, off = divmod(a * w, tile)
        row_loads.append(pltpu.make_async_copy(rows.at[a], rowv.at[j, :, :, pl.ds(off, w)], sems.at[4 + a]))
        row_loads[-1].start()

    def mat_in(i, j):
        return pltpu.make_async_copy(tile_at(mat, i, j), matv.at[i, j], mat_sem.at[i, j])

    loop(0, r_loc, lambda i: loop(0, c_loc, lambda j: mat_in(i, j).start()))

    for k in range(panels):
        rank = jnp.int32(0)
        for m in range(panels):
            rank += (piv[m] < piv[k]).astype(jnp.int32)
        slot[k] = rank

    def live(row, col):
        device = (col // c_loc) * rsize + row // r_loc
        return metas[device, (row % r_loc) * c_loc + col % c_loc]

    def kept(row, k):
        device = row // r_loc
        return metas[device, cells + (row % r_loc) * panels + k]

    for load in loads[:3]:
        load.wait()

    def split_inv(k):
        linvs[0, k], linvs[1, k] = halves(lv[k])
        uinvs[0, k], uinvs[1, k] = halves(uv[k])

    loop(0, panels, split_inv)

    def pair(ref, *index):
        return ref[(0,) + index], ref[(1,) + index]

    def cross_panel(k):
        def low(m):
            value = mm(halves(crossv[k, slot[m]]), pair(uinvs, k)) * kept(piv[m], k)
            lows[0, m, k], lows[1, m, k] = halves(value)

        def up(n):
            value = mm(pair(linvs, k), halves(crossv[n, slot[k]]))
            ups[0, k, n], ups[1, k, n] = halves(value)

        loop(k + 1, panels, low)
        loop(k + 1, panels, up)

        def update(m):
            def one(n):
                def go():
                    crossv[n, slot[m]] = crossv[n, slot[m]] - mm(pair(lows, m, k), pair(ups, k, n))

                when((m != n) & (live(piv[m], n * c_loc) != 0), go)

            loop(k + 1, panels, one)

        loop(k + 1, panels, update)

    loop(0, panels - 1, cross_panel)
    for load in row_loads:
        load.wait()

    def row_column(j):
        def panel(k):
            value = mm(pair(linvs, k), halves(rowv[j, slot[k]]))
            rowv[j, slot[k]] = value
            closed = (j == 0) & (plane <= k)
            shown = value * jnp.where(closed, 0.0, 1.0).astype(jnp.float32)
            at = pl.ds(pl.multiple_of(k * tile, tile), tile)
            us[0, j, at], us[1, j, at] = halves(shown)

            def update(m):
                def go():
                    seen = (us[0, j, at], us[1, j, at])
                    rowv[j, slot[m]] = rowv[j, slot[m]] - mm(pair(lows, m, k), seen)

                when(jnp.logical_not(closed) & (live(piv[m], plane * c_loc + j) != 0), go)

            loop(k + 1, panels, update)

        loop(0, panels, panel)

    loop(0, c_loc, row_column)
    loads[3].wait()

    def row_tile(i):
        at = pl.ds(pl.multiple_of(i * tile, tile), tile)
        row = me * r_loc + i
        for k in range(panels):
            gone = row == piv[0]
            for m in range(1, k + 1):
                gone = gone | (row == piv[m])
            keep = jnp.where(gone, 0.0, 1.0).astype(jnp.float32)
            value = mm(halves(stripv[k, at]), pair(uinvs, k)) * kept(row, k)
            lf[k] = value
            ls[0, :, k * tile : (k + 1) * tile], ls[1, :, k * tile : (k + 1) * tile] = halves(value * keep)

            def update(n, k=k):
                def go():
                    left = (ls[0, :, k * tile : (k + 1) * tile], ls[1, :, k * tile : (k + 1) * tile])
                    stripv[n, at] = stripv[n, at] - mm(left, pair(ups, k, n))

                when(live(row, n * c_loc) != 0, go)

            loop(k + 1, panels, update)

        loop(0, c_loc, lambda j: mat_in(i, j).wait())

        def target(j):
            def go():
                matv[i, j] = matv[i, j] - mm((ls[0], ls[1]), pair(us, j))

            when(live(row, plane * c_loc + j) != 0, go)

        loop(0, c_loc, target)
        for k in range(panels):
            gone = row == piv[0]
            for m in range(1, k + 1):
                gone = gone | (row == piv[m])

            def put_low(k=k):
                matv[i, 0] = lf[k]

            when((plane == k) & jnp.logical_not(gone), put_low)

            def put_up(k=k):
                def one(j):
                    def go():
                        matv[i, j] = rowv[j, slot[k]]

                    when((j != 0) | (plane > k), go)

                loop(0, c_loc, one)

            when(row == piv[k], put_up)

        loop(0, c_loc, lambda j: mat_out(i, j).start())

    def mat_out(i, j):
        return pltpu.make_async_copy(matv.at[i, j], tile_at(out, i, j), mat_sem.at[i, j])

    loop(0, r_loc, row_tile)
    loop(0, r_loc, lambda i: loop(0, c_loc, lambda j: mat_out(i, j).wait()))


def body(mesh, matrix, pattern, active, pivots, lower_inv, upper_inv):
    panels, tile = lower_inv.shape[:2]
    height, width = matrix.shape
    r_loc, c_loc = height // tile, width // tile
    rsize, csize = mesh.shape["row"], mesh.shape["col"]
    chips, w = rsize // 2, width // rsize
    dims = (panels, tile, r_loc, width, rsize, csize)
    devices = rsize * csize
    cells = r_loc * c_loc
    spot = active[0, 0, :, 0] * c_loc + active[0, 0, :, 1]
    live = jnp.any(spot[:, None] == jnp.arange(cells, dtype=jnp.int32)[None, :], axis=0)
    meta = jnp.concatenate([live.astype(jnp.float32), (pattern != 0).astype(jnp.float32).reshape(-1)])
    meta = jnp.broadcast_to(jnp.pad(meta, (0, 128 - meta.shape[0]))[None, :], (8, 128))
    f32, bf16 = jnp.float32, jnp.bfloat16
    picked = jnp.stack(ranked(pivots))
    mine = lax.axis_index("row") * r_loc + jnp.arange(r_loc, dtype=jnp.int32)
    hits = (picked[:, None] == mine[None, :]).astype(f32)
    any_spec = pl.BlockSpec(memory_space=pl.ANY)
    smem = pl.BlockSpec(memory_space=pltpu.SMEM)
    dma = pltpu.SemaphoreType.DMA
    rows, strips, cross, metas = pl.pallas_call(
        functools.partial(comm_kernel, dims, tuple(mesh.axis_names)),
        out_shape=[
            jax.ShapeDtypeStruct((rsize, panels, tile, w), f32),
            jax.ShapeDtypeStruct((panels, height, tile), f32),
            jax.ShapeDtypeStruct((panels, panels, tile, tile), f32),
            jax.ShapeDtypeStruct((devices, 8, 128), f32),
        ],
        in_specs=[smem, any_spec, any_spec],
        out_specs=[any_spec] * 4,
        scratch_shapes=[
            pltpu.VMEM((height, width), f32),
            pltpu.VMEM((2, chips, tile, w), f32),
            pltpu.VMEM((2, chips, tile, w), f32),
            pltpu.VMEM((2, chips, tile, w), f32),
            pltpu.VMEM((2, chips - 1, tile, w), f32),
            pltpu.VMEM((2, tile, w), f32),
            dma((devices,)), dma((devices,)),
            dma((2, panels, r_loc)), dma((2, panels, r_loc)),
            dma((panels, rsize)), dma((panels,)),
            dma((2,)), dma((2,)),
            dma((2, chips)), dma((2, chips)),
            dma((2, 2 * chips, panels)), dma((2, 2 * chips, panels)),
            dma((tile // w, rsize)), dma((tile // w,)),
            dma((csize,)), dma((panels,)),
            dma((6 + tile // w,)),
        ],
        compiler_params=pltpu.CompilerParams(has_side_effects=True),
        name="exchange",
    )(hits, meta, matrix)
    metas = metas[:, 0, :]
    return pl.pallas_call(
        functools.partial(lu_kernel, dims),
        out_shape=jax.ShapeDtypeStruct(matrix.shape, f32),
        in_specs=[smem, smem] + [any_spec] * 6,
        out_specs=any_spec,
        scratch_shapes=[
            pltpu.VMEM((r_loc, c_loc, tile, tile), f32),
            pltpu.VMEM((c_loc, panels, tile, tile), f32),
            pltpu.VMEM((panels, height, tile), f32),
            pltpu.VMEM((panels, panels, tile, tile), f32),
            pltpu.VMEM((panels, tile, tile), f32),
            pltpu.VMEM((panels, tile, tile), f32),
            pltpu.VMEM((2, panels, tile, tile), bf16),
            pltpu.VMEM((2, panels, tile, tile), bf16),
            pltpu.VMEM((2, panels, panels, tile, tile), bf16),
            pltpu.VMEM((2, panels, panels, tile, tile), bf16),
            pltpu.VMEM((2, c_loc, panels * tile, tile), bf16),
            pltpu.VMEM((2, tile, panels * tile), bf16),
            pltpu.VMEM((panels, tile, tile), f32),
            pltpu.SMEM((panels,), jnp.int32),
            dma((4 + rsize,)), dma((r_loc, c_loc)),
        ],
        compiler_params=pltpu.CompilerParams(vmem_limit_bytes=60 * 1024 * 1024),
        name="factor",
    )(pivots, metas, matrix, rows, strips, cross, lower_inv, upper_inv)


def solution(mesh):
    in_specs = (P("row", "col"), P("row", None), P("row", "col", None, None), P(), P(), P())
    return jax.shard_map(
        functools.partial(body, mesh),
        mesh=mesh,
        in_specs=in_specs,
        out_specs=P("row", "col"),
        check_vma=False,
    )
```

profile of v0, /device:TPU:0, one launch (start us, length us, event | category | flops | bytes accessed | tf_op | source)
XLA Modules:
  0.0 202.8 jit_solution(14094076133817926327)
XLA Ops:
  0.0 0.7 broadcast_compare_fusion
  0.7 0.1 reshape.33
  0.8 0.8 add_bitcast_fusion
  1.5 0.1 fusion
  1.6 0.1 pad_add_fusion
  1.7 1.5 fusion.1
  8.3 0.1 pad_add_fusion.1
  8.3 0.7 compare_convert_fusion.hits
  9.0 0.6 broadcast_in_dim.2.meta
  9.6 137.5 %exchange.1 = (f32[8,4,256,256]{3,2,1,0:T(8,128)}, f32[4,1024,256]{2,1,0:T(8,128)}, f32[4,4,256,256]{3,2,1,0:T(8,128)}, f32[32,8,128]{2,1,0:T(8,128)}) custom-call(f32[2,4]{1,0:T(2,128)} %compare_convert_fusion.hits, f32[8,128]{1,0:T(8,128)} %broadcast_in_dim.2.meta, f32[1024,2048]{1,0:T(8,128)} %mat.3), custom_call_target="tpu_custom_call" | custom-call | tf_op jit(solution)/shard_map/exchange/pallas_call | solution.py:542
  147.1 0.9 copy.8
  148.1 0.6 slice_bitcast_fusion.metas
  148.7 54.1 %factor.1 = f32[1024,2048]{1,0:T(8,128)} custom-call(s32[4]{0:T(128)} %piv.1, f32[32,128]{1,0:T(8,128)} %slice_bitcast_fusion.metas, f32[1024,2048]{1,0:T(8,128)} %mat.3, f32[8,4,256,256]{3,2,1,0:T(8,128)} %get-tuple-element.10.rows, f32[4,1024,256]{2,1,0:T(8,128)} %get-tuple-element.11.strips, f32[4,4,256,256]{3,2,1,0:T(8,128)} %get-tuple-element.12.cross, ...), custom_call_target="tpu_custom_call" | custom-call | tf_op jit(solution)/shard_map/factor/pallas_call | solution.py:573
  (2 shorter events, 0.0 us)
where the time goes:
time: 203 us
  Pallas kernels  192 us (95%)
  between operations  5.09 us (3%)
  local copies, waits for them, and re-layouts  3.68 us (2%)
  other arithmetic  2.36 us (1%)
    pallas_call x1, Pallas kernels, body(): pl.pallas_call(functools.partial(comm_kernel, dims, tuple(mesh.axis_names...  138 us
    pallas_call x1, Pallas kernels, body(): pl.pallas_call(functools.partial(lu_kernel, dims), out_shape=jax.ShapeDty...  54.1 us

commit v1 on v0

v1 whole, which is shorter than its diff:
```python
import functools

import jax
import jax.numpy as jnp
from jax import lax
from jax.experimental import pallas as pl
from jax.experimental.pallas import tpu as pltpu
from jax.sharding import PartitionSpec as P


def when(cond, fn):
    pl.when(cond)(fn)


def loop(low, high, fn):
    def one(index, carry):
        fn(index)
        return carry

    lax.fori_loop(low, high, one, 0)


def halves(value):
    high = value.astype(jnp.bfloat16)
    return high, (value - high.astype(jnp.float32)).astype(jnp.bfloat16)


def dot(left, right):
    return jnp.dot(left, right, preferred_element_type=jnp.float32)


def mm(left, right):
    (ah, al), (bh, bl) = left, right
    return dot(ah, bh) + dot(ah, bl) + dot(al, bh)


def pair(ref, *index):
    return ref[(0,) + index], ref[(1,) + index]


def lane(value, index):
    at = lax.broadcasted_iota(jnp.int32, value.shape, value.ndim - 1)
    return jnp.sum(jnp.where(at == index, value, 0.0), axis=-1, keepdims=True)


def exchange_kernel(
    dims, axes, ctl, piv, meta, mat, linv, uinv, rows, lows_out,
    matv, strips, cross, metas, sel, xcand, xgot, xfix, send1, recv1, buf2, recv2, homes, fixed_in, work,
    linvs, uinvs, lows, ups, done_low,
    m_send, m_recv, z_send, z_recv, xc_send, xc_recv, xf_send, xf_recv, ab_send, ab_recv, one_send, one_recv,
    two_send, two_recv, ag_send, ag_recv, xz_send, xz_recv, out_sem, local,
):
    panels, tile, r_loc, width, rsize, csize = dims
    c_loc = width // tile
    chips = rsize // 2
    w = width // rsize
    rr = tile // rsize
    last = panels - 1
    me = lax.axis_index("row")
    plane = lax.axis_index("col")
    chip, core = me // 2, me % 2
    lin = plane * rsize + me
    square = chips == 4
    is_holder = plane < panels

    def dev(row, col):
        return tuple(row if name == "row" else col for name in axes)

    def remote(src, dst, ssem, rsem, row, col):
        return pltpu.make_async_remote_copy(
            src_ref=src, dst_ref=dst, send_sem=ssem, recv_sem=rsem,
            device_id=dev(row, col), device_id_type=pl.DeviceIdType.MESH,
        )

    if square:
        x, y = chip % 2, chip // 2
        xn, yn = chip + 1 - 2 * x, chip + 2 - 4 * y
        to_chip = from_chip = [xn, yn, 3 - chip]
    else:
        to_chip = [(chip + d) % chips for d in range(1, chips)]
        from_chip = [(chip - d + chips) % chips for d in range(1, chips)]
    sib = chip * 2 + 1 - core

    def block(index, size):
        return pl.ds(pl.multiple_of(index * size, size), size)

    def z_own(r, up):
        return remote(
            mat.at[block(r, tile), pl.ds(0, tile)], strips.at[plane, r],
            z_send.at[1 - up, plane, r], z_recv.at[1 - up, plane, r], me, plane + 2 * up - 1,
        )

    def z_pass(n, r, up):
        return remote(
            strips.at[n, r], strips.at[n, r],
            z_send.at[1 - up, n, r], z_recv.at[1 - up, n, r], me, plane + 2 * up - 1,
        )

    def z_start(r):
        when(is_holder & (plane + 1 < csize), lambda: z_own(r, 1).start())
        when(is_holder & (plane > 0), lambda: z_own(r, 0).start())

    def z_relay(p, r):
        low, high = plane - p, plane + p

        def from_low():
            z_pass(low, r, 1).wait_recv()
            when(plane + 1 < csize, lambda: z_pass(low, r, 1).start())

        def from_high():
            z_pass(high, r, 0).wait_recv()
            when(plane > 0, lambda: z_pass(high, r, 0).start())

        when((low >= 0) & (low < panels), from_low)
        when(high < panels, from_high)

    def z_drain(p, r):
        low, high = plane - p, plane + p
        if p == 0:
            when(is_holder & (plane + 1 < csize), lambda: z_own(r, 1).wait_send())
            when(is_holder & (plane > 0), lambda: z_own(r, 0).wait_send())
        else:
            when((low >= 0) & (low < panels) & (plane + 1 < csize), lambda: z_pass(low, r, 1).wait_send())
            when((high < panels) & (plane > 0), lambda: z_pass(high, r, 0).wait_send())

    loop(0, 2, z_start)
    first_load = pltpu.make_async_copy(mat.at[:, pl.ds(0, tile)], matv.at[:, pl.ds(0, tile)], local.at[1])
    rest_load = pltpu.make_async_copy(
        mat.at[:, pl.ds(tile, width - tile)], matv.at[:, pl.ds(tile, width - tile)], local.at[2]
    )
    first_load.start()
    rest_load.start()

    def meta_copy(t):
        return remote(meta, metas.at[plane, me], m_send.at[t], m_recv.at[lin], t % rsize, t // rsize)

    def meta_in(t):
        return remote(
            meta, metas.at[t // rsize, t % rsize], m_send.at[t], m_recv.at[t], t % rsize, t // rsize
        )

    def x_give(a):
        return remote(
            xcand.at[:, block(a, rr), :], xgot.at[me], xc_send.at[a], xc_recv.at[me], a, plane
        )

    def x_got(a):
        return remote(xcand.at[:, block(a, rr), :], xgot.at[a], xc_send.at[a], xc_recv.at[a], a, plane)

    def x_fixed(slot):
        base = 0 if slot == 0 else (r_loc - 1) * tile

        def to(a):
            return remote(
                mat.at[pl.ds(pl.multiple_of(base + a * rr, rr), rr), pl.ds(0, tile)], xfix.at[slot],
                xf_send.at[slot, a], xf_recv.at[slot], a, plane,
            )

        return to

    x_top, x_bottom = x_fixed(0), x_fixed(1)
    step = 32

    def mix(values, weights):
        total = values[0] * weights[0]
        for value, weight in zip(values[1:], weights[1:]):
            total = total + value * weight
        return total

    first_load.wait()

    def x_pick(part):
        at = block(part, step)
        seen = [matv[pl.ds(pl.multiple_of(r * tile + part * step, step), step), :tile] for r in range(r_loc)]
        for s in range(2):
            xcand[s, at] = mix(seen, [ctl[s, r] for r in range(r_loc)])

    loop(0, tile // step, x_pick)

    def x_spread():
        when(me == 0, lambda: loop(1, rsize, lambda a: x_top(a).start()))
        when(me == rsize - 1, lambda: loop(0, rsize - 1, lambda a: x_bottom(a).start()))
        loop(0, rsize, lambda a: when(a != me, lambda: x_give(a).start()))

    when(is_holder, x_spread)
    loop(0, rsize * csize, lambda t: when(t != lin, lambda: meta_copy(t).start()))
    own_meta = pltpu.make_async_copy(meta, metas.at[plane, me], local.at[0])
    own_meta.start()

    def fixed(slot):
        base = 0 if slot == 0 else (r_loc - 1) * tile

        def to(a):
            return remote(
                mat.at[pl.ds(base, tile), block(a, w)], fixed_in.at[slot],
                ab_send.at[slot, a], ab_recv.at[slot], a, plane,
            )

        return to

    top, bottom = fixed(0), fixed(1)
    when(me == 0, lambda: loop(1, rsize, lambda a: top(a).start()))
    when(me == rsize - 1, lambda: loop(0, rsize - 1, lambda a: bottom(a).start()))
    high_core = (core == 0).astype(jnp.float32)
    low_core = 1.0 - high_core

    def one(s):
        return remote(send1.at[s], recv1.at[s], one_send.at[s], one_recv.at[s], sib, plane)

    def pick(part):
        at = block(part, step)
        for q in range(chips):
            even, odd = [], []
            for r in range(r_loc):
                there = pl.ds(pl.multiple_of(r * tile + part * step, step), step)
                even.append(matv[there, 2 * q * w : (2 * q + 1) * w])
                odd.append(matv[there, (2 * q + 1) * w : (2 * q + 2) * w])
            for s in range(2):
                weights = [ctl[s, r] for r in range(r_loc)]
                left, right = mix(even, weights), mix(odd, weights)
                send1[s, q, at] = left * low_core + right * high_core
                buf2[s, q, at] = left * high_core + right * low_core

    rest_load.wait()
    loop(0, tile // step, pick)
    for s in range(2):
        one(s).start()
    base = (r_loc - 1) * tile
    own_fixed = [
        pltpu.make_async_copy(matv.at[pl.ds(0, tile), pl.ds(0, w)], fixed_in.at[0], local.at[4]),
        pltpu.make_async_copy(
            matv.at[pl.ds(base, tile), pl.ds((rsize - 1) * w, w)], fixed_in.at[1], local.at[4]
        ),
    ]
    own_xfix = [
        pltpu.make_async_copy(matv.at[pl.ds(0, rr), pl.ds(0, tile)], xfix.at[0], local.at[5]),
        pltpu.make_async_copy(
            matv.at[pl.ds(base + (rsize - 1) * rr, rr), pl.ds(0, tile)], xfix.at[1], local.at[5]
        ),
    ]

    def own_z(r):
        return pltpu.make_async_copy(matv.at[block(r, tile), pl.ds(0, tile)], strips.at[plane, r], out_sem.at[r])

    for side, root in ((0, 0), (1, rsize - 1)):
        when(me == root, lambda side=side: own_fixed[side].start())
        when(is_holder & (me == root), lambda side=side: own_xfix[side].start())
    when(is_holder, lambda: loop(0, r_loc, lambda r: own_z(r).start()))

    def two(s, d):
        return remote(
            buf2.at[s, to_chip[d]], recv2.at[s, d], two_send.at[s, d], two_recv.at[s, d],
            to_chip[d] * 2 + core, plane,
        )

    def combine(s):
        one(s).wait_recv()
        for q in range(chips):
            buf2[s, q] = buf2[s, q] + recv1[s, q]

    combine(0)
    for d in range(chips - 1):
        two(0, d).start()

    def x_region(a, n):
        return cross.at[n, :, block(a, rr), :]

    def xz(d):
        return remote(
            x_region(me, plane), x_region(me, plane), xz_send.at[d], xz_recv.at[plane],
            me, (plane + d) % csize,
        )

    def x_home():
        for side, root in ((0, 0), (1, rsize - 1)):
            when(me != root, lambda side=side: (x_top if side == 0 else x_bottom)(me).wait_recv())
            when(me == root, lambda side=side: own_xfix[side].wait())
        loop(0, rsize, lambda a: when(a != me, lambda: x_got(a).wait_recv()))
        xgot[me] = xcand[:, block(me, rr), :]
        total = xgot[0]
        for a in range(1, rsize):
            total = total + xgot[a]
        slots = [xfix[0], total[0], total[1], xfix[1]]
        for k in range(panels):
            cross[plane, k, block(me, rr), :] = mix(slots, [ctl[k, r_loc + s] for s in range(panels)])
        loop(1, csize, lambda d: xz(d).start())

    when(is_holder, x_home)
    loop(2, r_loc, z_start)
    combine(1)

    def region(a, c):
        return rows.at[a, c]

    def ag(part, c, kind, a, row):
        ref = region(a, c) if part == 0 else x_region(a, c)
        return remote(ref, ref, ag_send.at[part, kind, c], ag_recv.at[part, kind, c], row, plane)

    direct = 2 if square else chips - 1
    sib_own = chips - 1
    half = panels // 2

    def peer(d):
        return from_chip[d] * 2 + core

    def ag_start(part, c):
        for d in range(direct):
            ag(part, c, d, me, to_chip[d] * 2 + core).start()
        ag(part, c, sib_own, me, sib).start()

    def ag_forward(part, c, first):
        for d in range(direct):
            ag(part, c, d, peer(d), sib).wait_recv()
            if square and first == (d == 0):
                ag(part, c, 2, peer(d), to_chip[1 - d] * 2 + core).start()
            ag(part, c, chips + d, peer(d), sib).start()

    def ag_far(part, c):
        if square:
            ag(part, c, 2, peer(2), sib).wait_recv()
            ag(part, c, chips + 2, peer(2), sib).start()

    def ag_in(part, c):
        for d in range(chips):
            kind = sib_own if d == chips - 1 else chips + d
            ag(part, c, kind, sib if d == chips - 1 else from_chip[d] * 2 + 1 - core, sib).wait_recv()

    def ag_out(part, c, first):
        ag(part, c, sib_own, me, sib).wait_send()
        for d in range(direct):
            ag(part, c, d, me, to_chip[d] * 2 + core).wait_send()
        for d in range(chips - 1):
            ag(part, c, chips + d, peer(d), sib).wait_send()
        if square:
            d = 0 if first else 1
            ag(part, c, 2, peer(d), to_chip[1 - d] * 2 + core).wait_send()

    def halved(fn):
        loop(0, half, lambda c: fn(c, True))
        loop(half, panels, lambda c: fn(c, False))

    def x_start(n):
        got = remote(x_region(me, n), x_region(me, n), xz_send.at[0], xz_recv.at[n], me, plane)
        when(plane != n, lambda: got.wait_recv())
        ag_start(1, n)

    loop(0, panels, x_start)
    for d in range(chips - 1):
        two(1, d).start()
    for r in range(2):
        z_relay(1, r)
    halved(lambda c, first: ag_forward(1, c, first))
    loop(2, r_loc, lambda r: z_relay(1, r))
    loop(0, panels, lambda c: ag_far(1, c))

    def split_inv(k):
        linvs[0, k], linvs[1, k] = halves(linv[k])
        uinvs[0, k], uinvs[1, k] = halves(uinv[k])

    loop(0, panels, split_inv)
    own_meta.wait()

    def meta_end(t):
        meta_copy(t).wait_send()
        meta_in(t).wait_recv()

    loop(0, rsize * csize, lambda t: when(t != lin, lambda: meta_end(t)))
    at_row = lax.broadcasted_iota(jnp.int32, (rsize, 8, 128), 0)
    at_sub = lax.broadcasted_iota(jnp.int32, (rsize, 8, 128), 1)
    ids = jnp.where(at_sub < r_loc, at_row * r_loc + at_sub, -1)
    for m in range(panels):
        chosen = jnp.where(ids == piv[m], 1.0, 0.0)

        def gather(n, m=m, chosen=chosen):
            found = jnp.sum(jnp.sum(chosen * metas[n], axis=0), axis=0, keepdims=True)
            sel[m, n] = found

        loop(0, csize, gather)
    loop(0, panels, lambda c: ag_in(1, c))
    halved(lambda c, first: ag_out(1, c, first))
    when(is_holder, lambda: loop(1, csize, lambda d: xz(d).wait_send()))

    def cross_panel(k):
        def low(m):
            value = mm(halves(cross[k, m]), pair(uinvs, k)) * lane(sel[m, 0], c_loc + k)
            lows[0, m, k], lows[1, m, k] = halves(value)

        def up(n):
            value = mm(pair(linvs, k), halves(cross[n, k]))
            ups[0, k, n], ups[1, k, n] = halves(value)

        loop(k + 1, panels, low)
        loop(k + 1, panels, up)

        def update(m):
            def one_tile(n):
                def go():
                    product = mm(pair(lows, m, k), pair(ups, k, n)) * lane(sel[m, n], 0)
                    cross[n, m] = cross[n, m] - product

                when(m != n, go)

            loop(k + 1, panels, one_tile)

        loop(k + 1, panels, update)

    loop(0, panels - 1, cross_panel)

    for s in range(2):
        total = buf2[s, chip]
        for d in range(chips - 1):
            two(s, d).wait_recv()
            total = total + recv2[s, d]
        homes[s] = total
    for side, root in ((0, 0), (1, rsize - 1)):
        when(me != root, lambda side=side: (top if side == 0 else bottom)(me).wait_recv())
        when(me == root, lambda side=side: own_fixed[side].wait())

    def order(part):
        at = block(part, step)
        slots = [fixed_in[0, at], homes[0, at], homes[1, at], fixed_in[1, at]]
        for k in range(panels):
            work[k, at, :w] = mix(slots, [ctl[k, r_loc + s] for s in range(panels)])

    loop(0, tile // step, order)
    column = (me * w) // tile

    def put(k):
        return pltpu.make_async_copy(work.at[k, :, pl.ds(0, w)], rows.at[me, k], local.at[6])

    def home_panel(k):
        value = mm(pair(linvs, k), halves(work[k, :, :w]))
        work[k, :, :w] = value
        put(k).start()
        opened = 1.0 - ((column == 0) & (plane <= k)).astype(jnp.float32)
        seen = halves(value)

        def update(m):
            product = mm(pair(lows, m, k), seen) * (lane(sel[m, plane], column) * opened)
            work[m, :, :w] = work[m, :, :w] - product

        loop(k + 1, panels, update)
        put(k).wait()
        ag_start(0, k)

    loop(0, panels, home_panel)

    def column_tile(r):
        def panel(k):
            value = mm(halves(work[k]), pair(uinvs, k)) * lane(meta[pl.ds(r, 1), :], c_loc + k)
            done_low[r, k] = value
            seen = halves(value * ctl[k, r_loc + panels + r])

            def update(n):
                product = mm(seen, pair(ups, k, n)) * lane(metas[n, me, pl.ds(r, 1), :], 0)
                work[n] = work[n] - product

            loop(k + 1, panels, update)

        def fetch(k):
            work[k] = strips[k, r]

        loop(0, panels, fetch)
        loop(0, panels, panel)

    def low_out(r):
        return pltpu.make_async_copy(done_low.at[r], lows_out.at[r], out_sem.at[r])

    when(is_holder, lambda: loop(0, r_loc, lambda r: own_z(r).wait()))

    def serve(r):
        for p in range(2, csize):
            z_relay(p, r)
        column_tile(r)
        low_out(r).start()

    for c in range(max(panels, r_loc)):
        if c < panels:
            ag_forward(0, c, c < half)
        if c < r_loc:
            loop(c, c + 1, serve)
    loop(0, panels, lambda c: ag_far(0, c))
    loop(0, panels, lambda c: ag_in(0, c))
    halved(lambda c, first: ag_out(0, c, first))
    for p in range(csize):
        loop(0, r_loc, lambda r, p=p: z_drain(p, r))
    for s in range(2):
        one(s).wait_send()
        for d in range(chips - 1):
            two(s, d).wait_send()
    when(me == 0, lambda: loop(1, rsize, lambda a: top(a).wait_send()))
    when(me == rsize - 1, lambda: loop(0, rsize - 1, lambda a: bottom(a).wait_send()))

    def x_spread_end():
        when(me == 0, lambda: loop(1, rsize, lambda a: x_top(a).wait_send()))
        when(me == rsize - 1, lambda: loop(0, rsize - 1, lambda a: x_bottom(a).wait_send()))
        loop(0, rsize, lambda a: when(a != me, lambda: x_give(a).wait_send()))

    when(is_holder, x_spread_end)
    loop(0, r_loc, lambda r: low_out(r).wait())


def final_kernel(dims, piv, meta, mat, rows, lows, out, matv, rowv, lowv, us, ls, row_sem, low_sem, mat_sem):
    panels, tile, r_loc, width, rsize, csize = dims
    c_loc = width // tile
    w = width // rsize
    me = lax.axis_index("row")
    plane = lax.axis_index("col")

    def tile_at(ref, i, j):
        return ref.at[pl.ds(pl.multiple_of(i * tile, tile), tile), pl.ds(pl.multiple_of(j * tile, tile), tile)]

    row_loads = []
    for a in range(rsize):
        j, off = divmod(a * w, tile)
        row_loads.append(pltpu.make_async_copy(rows.at[a], rowv.at[j, :, :, pl.ds(off, w)], row_sem.at[a]))

    def low_in(i):
        return pltpu.make_async_copy(lows.at[i], lowv.at[i], low_sem.at[i])

    def mat_in(i, j):
        return pltpu.make_async_copy(tile_at(mat, i, j), matv.at[i, j], mat_sem.at[i, j])

    def mat_out(i, j):
        return pltpu.make_async_copy(matv.at[i, j], tile_at(out, i, j), mat_sem.at[i, j])

    loop(0, 1, lambda i: low_in(i).start())
    for load in row_loads:
        load.start()
    loop(1, r_loc, lambda i: low_in(i).start())
    loop(0, r_loc, lambda i: loop(0, c_loc, lambda j: mat_in(i, j).start()))

    def gone_at(row, k):
        gone = row == piv[0]
        for m in range(1, k + 1):
            gone = gone | (row == piv[m])
        return gone

    def row_tile(i):
        low_in(i).wait()
        row = me * r_loc + i
        for k in range(panels):
            keep = jnp.where(gone_at(row, k), 0.0, 1.0).astype(jnp.float32)
            span = slice(k * tile, (k + 1) * tile)
            ls[0, :, span], ls[1, :, span] = halves(lowv[i, k] * keep)

        def target(j):
            mat_in(i, j).wait()

            def go():
                matv[i, j] = matv[i, j] - mm((ls[0], ls[1]), pair(us, j))

            when(meta[i, j] != 0, go)

        loop(0, c_loc, target)
        for k in range(panels):

            def put_low(k=k):
                matv[i, 0] = lowv[i, k]

            when((plane == k) & jnp.logical_not(gone_at(row, k)), put_low)

            def put_up(k=k):
                def one(j):
                    def go():
                        matv[i, j] = rowv[j, k]

                    when((j != 0) | (plane > k), go)

                loop(0, c_loc, one)

            when(row == piv[k], put_up)

        loop(0, c_loc, lambda j: mat_out(i, j).start())

    for load in row_loads:
        load.wait()

    def split_up(j):
        for k in range(panels):
            shown = jnp.where((j == 0) & (plane <= k), 0.0, 1.0).astype(jnp.float32)
            us[0, j, k * tile : (k + 1) * tile], us[1, j, k * tile : (k + 1) * tile] = halves(rowv[j, k] * shown)

    loop(0, c_loc, split_up)
    loop(0, r_loc, row_tile)
    loop(0, r_loc, lambda i: loop(0, c_loc, lambda j: mat_out(i, j).wait()))


def body(mesh, matrix, pattern, active, pivots, lower_inv, upper_inv):
    panels, tile = lower_inv.shape[:2]
    height, width = matrix.shape
    r_loc, c_loc = height // tile, width // tile
    rsize, csize = mesh.shape["row"], mesh.shape["col"]
    chips, w = rsize // 2, width // rsize
    rr = tile // rsize
    dims = (panels, tile, r_loc, width, rsize, csize)
    devices = rsize * csize
    f32, bf16 = jnp.float32, jnp.bfloat16

    spot = active[0, 0, :, 0] * 128 + active[0, 0, :, 1]
    places = jnp.arange(8, dtype=jnp.int32)[:, None] * 128 + jnp.arange(128, dtype=jnp.int32)[None, :]
    live = jnp.any(spot[:, None, None] == places[None], axis=0).astype(f32)
    kept = jnp.pad((pattern != 0).astype(f32), ((0, 8 - r_loc), (c_loc, 128 - c_loc - panels)))
    meta = live + kept
    ranks = jnp.sum((pivots[None, :] < pivots[:, None]).astype(jnp.int32), axis=1)
    order = ranks[:, None] == jnp.arange(panels, dtype=jnp.int32)[None, :]
    mine = lax.axis_index("row") * r_loc + jnp.arange(r_loc, dtype=jnp.int32)
    here = pivots[:, None] == mine[None, :]
    hits = jnp.any(order[:, 1:-1, None] & here[:, None, :], axis=0)
    hits = jnp.pad(hits, ((0, panels - hits.shape[0]), (0, 0)))
    upto = jnp.arange(panels)[:, None] >= jnp.arange(panels)[None, :]
    open_rows = jnp.logical_not(jnp.any(upto[:, :, None] & here[None], axis=1))
    ctl = jnp.concatenate([hits, order, open_rows], axis=1).astype(f32)

    any_spec = pl.BlockSpec(memory_space=pl.ANY)
    smem = pl.BlockSpec(memory_space=pltpu.SMEM)
    vmem = pl.BlockSpec(memory_space=pltpu.VMEM)
    dma = pltpu.SemaphoreType.DMA
    rows, lows = pl.pallas_call(
        functools.partial(exchange_kernel, dims, tuple(mesh.axis_names)),
        out_shape=[
            jax.ShapeDtypeStruct((rsize, panels, tile, w), f32),
            jax.ShapeDtypeStruct((r_loc, panels, tile, tile), f32),
        ],
        in_specs=[smem, smem, vmem, any_spec, vmem, vmem],
        out_specs=[any_spec] * 2,
        scratch_shapes=[
            pltpu.VMEM((height, width), f32),
            pltpu.VMEM((panels, r_loc, tile, tile), f32),
            pltpu.VMEM((panels, panels, tile, tile), f32),
            pltpu.VMEM((csize, rsize, 8, 128), f32),
            pltpu.VMEM((panels, csize, 1, 128), f32),
            pltpu.VMEM((2, tile, tile), f32),
            pltpu.VMEM((rsize, 2, rr, tile), f32),
            pltpu.VMEM((2, rr, tile), f32),
            pltpu.VMEM((2, chips, tile, w), f32),
            pltpu.VMEM((2, chips, tile, w), f32),
            pltpu.VMEM((2, chips, tile, w), f32),
            pltpu.VMEM((2, chips - 1, tile, w), f32),
            pltpu.VMEM((2, tile, w), f32),
            pltpu.VMEM((2, tile, w), f32),
            pltpu.VMEM((panels, tile, tile), f32),
            pltpu.VMEM((2, panels, tile, tile), bf16),
            pltpu.VMEM((2, panels, tile, tile), bf16),
            pltpu.VMEM((2, panels, panels, tile, tile), bf16),
            pltpu.VMEM((2, panels, panels, tile, tile), bf16),
            pltpu.VMEM((r_loc, panels, tile, tile), f32),
            dma((devices,)), dma((devices,)),
            dma((2, panels, r_loc)), dma((2, panels, r_loc)),
            dma((rsize,)), dma((rsize,)),
            dma((2, rsize)), dma((2,)),
            dma((2, rsize)), dma((2,)),
            dma((2,)), dma((2,)),
            dma((2, chips)), dma((2, chips)),
            dma((2, 2 * chips, panels)), dma((2, 2 * chips, panels)),
            dma((csize,)), dma((panels,)),
            dma((r_loc,)), dma((7,)),
        ],
        compiler_params=pltpu.CompilerParams(has_side_effects=True, vmem_limit_bytes=58 * 1024 * 1024),
        name="exchange",
    )(ctl, pivots, meta, matrix, lower_inv, upper_inv)
    return pl.pallas_call(
        functools.partial(final_kernel, dims),
        out_shape=jax.ShapeDtypeStruct(matrix.shape, f32),
        in_specs=[smem, smem] + [any_spec] * 3,
        out_specs=any_spec,
        scratch_shapes=[
            pltpu.VMEM((r_loc, c_loc, tile, tile), f32),
            pltpu.VMEM((c_loc, panels, tile, tile), f32),
            pltpu.VMEM((r_loc, panels, tile, tile), f32),
            pltpu.VMEM((2, c_loc, panels * tile, tile), bf16),
            pltpu.VMEM((2, tile, panels * tile), bf16),
            dma((rsize,)), dma((r_loc,)), dma((r_loc, c_loc)),
        ],
        compiler_params=pltpu.CompilerParams(vmem_limit_bytes=58 * 1024 * 1024),
        name="final",
    )(pivots, meta, matrix, rows, lows)


def solution(mesh):
    in_specs = (P("row", "col"), P("row", None), P("row", "col", None, None), P(), P(), P())
    return jax.shard_map(
        functools.partial(body, mesh),
        mesh=mesh,
        in_specs=in_specs,
        out_specs=P("row", "col"),
        check_vma=False,
    )
```

time: 203 us -> 151 us (0.74)
  Pallas kernels: 192 us -> 146 us
  between operations: 5.09 us -> 0.02 us
  local copies, waits for them, and re-layouts: 3.68 us -> 0.19 us
  other arithmetic: 2.36 us -> 4.84 us
    pallas_call x2, Pallas kernels: 192 us -> 146 us  [the longest x1 122 us: body(): pl.pallas_call(functools.partial(exchange_kernel, dims, tuple(mesh.axis_n...]
where the time goes in v1:
time: 151 us
  Pallas kernels  146 us (97%)
  other arithmetic  4.84 us (3%)
    pallas_call x1, Pallas kernels, body(): pl.pallas_call(functools.partial(exchange_kernel, dims, tuple(mesh.axis_n...  122 us
    pallas_call x1, Pallas kernels, body(): pl.pallas_call(functools.partial(final_kernel, dims), out_shape=jax.Shape...  23.3 us

profile of v1, /device:TPU:0, one launch (start us, length us, event | category | flops | bytes accessed | tf_op | source)
XLA Modules:
  0.0 150.7 jit_solution(16787183022168758948)
XLA Ops:
  0.0 0.7 broadcast_compare_fusion.1
  0.7 0.8 add_bitcast_fusion
  1.4 0.9 convert_reduce_fusion
  2.4 0.1 iota_compare_fusion.1
  2.4 0.1 slice.11
  2.5 0.1 copy.7
  2.6 0.7 iota_compare_fusion
  3.4 0.1 and_reduce_fusion
  3.5 0.1 and_reduce_fusion.1
  3.5 0.7 fusion.1.ctl
  4.2 0.1 iota_add_fusion
  4.3 0.1 compare_reduce_fusion
  4.4 0.7 convert_add_fusion.meta
  5.0 122.3 %exchange.1 = (f32[8,4,256,256]{3,2,1,0:T(8,128)}, f32[4,4,256,256]{3,2,1,0:T(8,128)}) custom-call(f32[4,12]{1,0:T(4,128)} %fusion.1.ctl, s32[4]{0:T(128)} %piv.3, f32[8,128]{1,0:T(8,128)} %convert_add_fusion.meta, f32[1024,2048]{1,0:T(8,128)} %mat.3, f32[4,256,256]{2,1,0:T(8,128)} %linv.1, f32[4,256,256]{2,1,0:T(8,128)} %uinv.1), custom_call_target="tpu_custom_call" | custom-call | tf_op jit(solution)/shard_map/exchange/pallas_call | solution.py:619
  127.4 23.3 %final.1 = f32[1024,2048]{1,0:T(8,128)} custom-call(s32[4]{0:T(128)} %piv.3, f32[8,128]{1,0:T(8,128)} %convert_add_fusion.meta, f32[1024,2048]{1,0:T(8,128)} %mat.3, f32[8,4,256,256]{3,2,1,0:T(8,128)} %get-tuple-element.7.rows, f32[4,4,256,256]{3,2,1,0:T(8,128)} %get-tuple-element.8.lows), custom_call_target="tpu_custom_call" | custom-call | tf_op jit(solution)/shard_map/final/pallas_call | solution.py:662
  (3 shorter events, 0.0 us)

commit v2 on v1

--- a/solution.py
+++ b/solution.py
@@ -262,6 +262,9 @@
     for d in range(chips - 1):
         two(0, d).start()
 
+    def spot(n, m):
+        return (m - n + panels - 1) % panels
+
     def x_region(a, n):
         return cross.at[n, :, block(a, rr), :]
 
@@ -282,7 +285,12 @@
             total = total + xgot[a]
         slots = [xfix[0], total[0], total[1], xfix[1]]
         for k in range(panels):
-            cross[plane, k, block(me, rr), :] = mix(slots, [ctl[k, r_loc + s] for s in range(panels)])
+
+            def keep(k=k):
+                mixed = mix(slots, [ctl[k, r_loc + s] for s in range(panels)])
+                cross[plane, spot(plane, k), block(me, rr), :] = mixed
+
+            when(plane != k, keep)
         loop(1, csize, lambda d: xz(d).start())
 
     when(is_holder, x_home)
@@ -345,11 +353,11 @@
         ag_start(1, n)
 
     loop(0, panels, x_start)
-    for d in range(chips - 1):
-        two(1, d).start()
     for r in range(2):
         z_relay(1, r)
     halved(lambda c, first: ag_forward(1, c, first))
+    for d in range(chips - 1):
+        two(1, d).start()
     loop(2, r_loc, lambda r: z_relay(1, r))
     loop(0, panels, lambda c: ag_far(1, c))
 
@@ -382,11 +390,11 @@
 
     def cross_panel(k):
         def low(m):
-            value = mm(halves(cross[k, m]), pair(uinvs, k)) * lane(sel[m, 0], c_loc + k)
+            value = mm(halves(cross[k, spot(k, m)]), pair(uinvs, k)) * lane(sel[m, 0], c_loc + k)
             lows[0, m, k], lows[1, m, k] = halves(value)
 
         def up(n):
-            value = mm(pair(linvs, k), halves(cross[n, k]))
+            value = mm(pair(linvs, k), halves(cross[n, spot(n, k)]))
             ups[0, k, n], ups[1, k, n] = halves(value)
 
         loop(k + 1, panels, low)
@@ -396,7 +404,7 @@
             def one_tile(n):
                 def go():
                     product = mm(pair(lows, m, k), pair(ups, k, n)) * lane(sel[m, n], 0)
-                    cross[n, m] = cross[n, m] - product
+                    cross[n, spot(n, m)] = cross[n, spot(n, m)] - product
 
                 when(m != n, go)
 
@@ -405,6 +413,7 @@
         loop(k + 1, panels, update)
 
     loop(0, panels - 1, cross_panel)
+    loop(0, 2, lambda r: z_relay(2, r))
 
     for s in range(2):
         total = buf2[s, chip]
@@ -444,6 +453,7 @@
         ag_start(0, k)
 
     loop(0, panels, home_panel)
+    loop(2, r_loc, lambda r: z_relay(2, r))
 
     def column_tile(r):
         def panel(k):
@@ -469,7 +479,7 @@
     when(is_holder, lambda: loop(0, r_loc, lambda r: own_z(r).wait()))
 
     def serve(r):
-        for p in range(2, csize):
+        for p in range(3, csize):
             z_relay(p, r)
         column_tile(r)
         low_out(r).start()
@@ -627,7 +637,7 @@
         scratch_shapes=[
             pltpu.VMEM((height, width), f32),
             pltpu.VMEM((panels, r_loc, tile, tile), f32),
-            pltpu.VMEM((panels, panels, tile, tile), f32),
+            pltpu.VMEM((panels, panels - 1, tile, tile), f32),
             pltpu.VMEM((csize, rsize, 8, 128), f32),
             pltpu.VMEM((panels, csize, 1, 128), f32),
             pltpu.VMEM((2, tile, tile), f32),

time: 151 us -> 141 us (0.934)
  Pallas kernels: 146 us -> 136 us
    pallas_call x1, Pallas kernels: 122 us -> 112 us  [body(): pl.pallas_call(functools.partial(exchange_kernel, dims, tuple(mesh.axis_n...]
where the time goes in v2:
time: 141 us
  Pallas kernels  136 us (96%)
  other arithmetic  4.84 us (3%)
    pallas_call x1, Pallas kernels, body(): pl.pallas_call(functools.partial(exchange_kernel, dims, tuple(mesh.axis_n...  112 us
    pallas_call x1, Pallas kernels, body(): pl.pallas_call(functools.partial(final_kernel, dims), out_shape=jax.Shape...  23.3 us

profile of v2, /device:TPU:0, one launch (start us, length us, event | category | flops | bytes accessed | tf_op | source)
XLA Modules:
  0.0 140.9 jit_solution(6846892438314281632)
XLA Ops:
  0.0 0.7 broadcast_compare_fusion.1
  0.7 0.8 add_bitcast_fusion
  1.4 0.9 convert_reduce_fusion
  2.4 0.1 iota_compare_fusion.1
  2.4 0.1 slice.11
  2.5 0.1 copy.7
  2.6 0.7 iota_compare_fusion
  3.4 0.1 and_reduce_fusion
  3.5 0.1 and_reduce_fusion.1
  3.5 0.7 fusion.1.ctl
  4.2 0.1 iota_add_fusion
  4.3 0.1 compare_reduce_fusion
  4.4 0.7 convert_add_fusion.meta
  5.0 112.5 %exchange.1 = (f32[8,4,256,256]{3,2,1,0:T(8,128)}, f32[4,4,256,256]{3,2,1,0:T(8,128)}) custom-call(f32[4,12]{1,0:T(4,128)} %fusion.1.ctl, s32[4]{0:T(128)} %piv.3, f32[8,128]{1,0:T(8,128)} %convert_add_fusion.meta, f32[1024,2048]{1,0:T(8,128)} %mat.3, f32[4,256,256]{2,1,0:T(8,128)} %linv.1, f32[4,256,256]{2,1,0:T(8,128)} %uinv.1), custom_call_target="tpu_custom_call" | custom-call | tf_op jit(solution)/shard_map/exchange/pallas_call | solution.py:629
  117.5 23.3 %final.1 = f32[1024,2048]{1,0:T(8,128)} custom-call(s32[4]{0:T(128)} %piv.3, f32[8,128]{1,0:T(8,128)} %convert_add_fusion.meta, f32[1024,2048]{1,0:T(8,128)} %mat.3, f32[8,4,256,256]{3,2,1,0:T(8,128)} %get-tuple-element.7.rows, f32[4,4,256,256]{3,2,1,0:T(8,128)} %get-tuple-element.8.lows), custom_call_target="tpu_custom_call" | custom-call | tf_op jit(solution)/shard_map/final/pallas_call | solution.py:672
  (3 shorter events, 0.0 us)
